TPU v7x, 32 devices: a whole 2x2x4 slice. The times are simulated.
32 devices in a mesh: ctx: 8 (over y, x, core), ch: 4 (over z).
Axes of the slice: x: 2, y: 2, z: 4, core: 2. Of those that a mesh axis runs over, the one named last changes fastest.
Arguments:
- queries: bfloat16 [8192, 2048], P('ch', 'ctx'), may hold values from -6 to 6
- keys: bfloat16 [8192, 2048], P('ch', 'ctx'), may hold values from -6 to 6
- values: bfloat16 [8192, 2048], P('ch', 'ctx'), may hold values from -6 to 6
- short_taps: float32 [3, 7, 8192], P(None, None, 'ch'), may hold values from -2 to 2
- long_filter: bfloat16 [4, 2048, 2048], P('ch', 'ctx'), may hold values from -1.5 to 1.5
- skip_gain: float32 [4, 2048], P('ch', 'ctx'), may hold values from 0.5 to 1.5
Outputs:
- mixed: bfloat16 [8192, 2048], P('ch', 'ctx')
All inputs are finite; a program needn't handle non-finite values.
Results may differ from a plain program's by a relative error of at most 0.01.
Values may be sent and summed in bfloat16 or wider, within the bound.
A program may use at most 64 MiB of HBM per device.

v0:
```python
import math
import jax
import jax.numpy as jnp
from jax import lax
from jax.sharding import PartitionSpec as P

HIGH = lax.Precision.HIGHEST


def passed_along(value, axis, by):
    peers = lax.axis_size(axis)
    pairs = [(i, i + by) for i in range(peers) if 0 <= i + by < peers]
    return lax.ppermute(value, axis, pairs)


def short_conv(extended, taps, length):
    rim = taps.shape[0] - 1
    total = jnp.zeros((extended.shape[0], length), jnp.float32)
    for shift_j in range(taps.shape[0]):
        total = total + taps[shift_j][:, None] * extended[:, rim - shift_j : rim - shift_j + length]
    return total


def split_table(table):
    table_head = table.astype(jnp.bfloat16)
    table_rest = (table - table_head.astype(jnp.float32)).astype(jnp.bfloat16)
    return (table_head, table_rest)


def long_conv(gated, filters, skips):
    channels, length = gated.shape
    size = 2 * length
    cols = 128
    rows = size // cols
    half = rows // 2
    two_pi = 2.0 * math.pi
    row_idx = jnp.arange(rows, dtype=jnp.int32)
    half_idx = jnp.arange(half, dtype=jnp.int32)
    col_idx = jnp.arange(cols, dtype=jnp.int32)
    angle_rows = two_pi * (row_idx[:, None] * half_idx[None, :] % rows).astype(jnp.float32) / rows
    cos_rows, sin_rows = (jnp.cos(angle_rows), jnp.sin(angle_rows))
    cos_head, cos_rest = split_table(cos_rows)
    sin_head, sin_rest = split_table(sin_rows)
    angle_twist = two_pi * (row_idx[:, None] * col_idx[None, :]).astype(jnp.float32) / size
    cos_twist, sin_twist = (jnp.cos(angle_twist), jnp.sin(angle_twist))
    angle_cols = two_pi * (col_idx[:, None] * col_idx[None, :] % cols).astype(jnp.float32) / cols
    cos_cols, sin_cols = (jnp.cos(angle_cols), jnp.sin(angle_cols))

    def first_section(table_head, table_rest, shaped):
        return jnp.einsum(
            "ka,cab->ckb", table_head, shaped, preferred_element_type=jnp.float32
        ) + jnp.einsum("ka,cab->ckb", table_rest, shaped, preferred_element_type=jnp.float32)

    def forward(signal):
        blocks = signal.shape[0]
        shaped = signal.reshape(blocks, half, cols)
        first_re = first_section(cos_head, cos_rest, shaped)
        first_im = -first_section(sin_head, sin_rest, shaped)
        twist_re = first_re * cos_twist + first_im * sin_twist
        twist_im = first_im * cos_twist - first_re * sin_twist
        out_re = jnp.einsum("ckb,bm->ckm", twist_re, cos_cols, precision=HIGH) + jnp.einsum(
            "ckb,bm->ckm", twist_im, sin_cols, precision=HIGH
        )
        out_im = jnp.einsum("ckb,bm->ckm", twist_im, cos_cols, precision=HIGH) - jnp.einsum(
            "ckb,bm->ckm", twist_re, sin_cols, precision=HIGH
        )
        return (out_re, out_im)

    def inverse(spec_re, spec_im):
        blocks = spec_re.shape[0]
        back_re = jnp.einsum("ckm,mb->ckb", spec_re, cos_cols, precision=HIGH) - jnp.einsum(
            "ckm,mb->ckb", spec_im, sin_cols, precision=HIGH
        )
        back_im = jnp.einsum("ckm,mb->ckb", spec_im, cos_cols, precision=HIGH) + jnp.einsum(
            "ckm,mb->ckb", spec_re, sin_cols, precision=HIGH
        )
        turn_re = back_re * cos_twist - back_im * sin_twist
        turn_im = back_re * sin_twist + back_im * cos_twist
        result = jnp.einsum("ka,ckb->cab", cos_rows, turn_re, precision=HIGH) - jnp.einsum(
            "ka,ckb->cab", sin_rows, turn_im, precision=HIGH
        )
        return (result / size).reshape(blocks, length)

    block = math.gcd(channels, 16)
    count = channels // block

    def one_block(triple):
        sig, filt, gain = triple
        sig_re, sig_im = forward(sig)
        filt_re, filt_im = forward(filt)
        prod_re = sig_re * filt_re - sig_im * filt_im
        prod_im = sig_re * filt_im + sig_im * filt_re
        return inverse(prod_re, prod_im) + gain[:, None] * sig.astype(jnp.float32)

    outcome = lax.map(
        one_block,
        (
            gated.reshape(count, block, length),
            filters.reshape(count, block, length),
            skips.reshape(count, block),
        ),
    )
    return outcome.reshape(channels, length).astype(jnp.bfloat16)


def gate_product(first, second):
    return (first.astype(jnp.float32) * second.astype(jnp.float32)).astype(jnp.bfloat16)


def local(queries, keys, values, short_taps, long_filter, skip_gain):
    width, tok_local = queries.shape
    rim = short_taps.shape[1] - 1
    stacked = jnp.stack(
        [queries[:, tok_local - rim :], keys[:, tok_local - rim :], values[:, tok_local - rim :]]
    )
    before = passed_along(stacked, "ctx", 1)

    def extend_home(source, which):
        return jnp.concatenate([before[which], source], axis=1).astype(jnp.float32)

    q_short = short_conv(extend_home(queries, 0), short_taps[0], tok_local).astype(jnp.bfloat16)
    gated = (
        short_conv(extend_home(keys, 1), short_taps[1], tok_local)
        * short_conv(extend_home(values, 2), short_taps[2], tok_local)
    ).astype(jnp.bfloat16)
    g_owned = lax.all_to_all(gated, "ctx", split_axis=0, concat_axis=1, tiled=True)
    outgoing = long_conv(g_owned, long_filter[0], skip_gain[0])
    returned = lax.all_to_all(outgoing, "ctx", split_axis=1, concat_axis=0, tiled=True)
    return gate_product(q_short, returned)


def solution(mesh):
    placed = (
        P("ch", "ctx"),
        P("ch", "ctx"),
        P("ch", "ctx"),
        P(None, None, "ch"),
        P("ch", "ctx", None),
        P("ch", "ctx"),
    )
    return jax.shard_map(
        local, mesh=mesh, in_specs=placed, out_specs=P("ch", "ctx"), check_vma=False
    )
```

profile of v0, /device:TPU:0, one launch (start us, length us, event | category | flops | bytes accessed | tf_op | source)
XLA Modules:
  0.0 269.8 jit_solution(2288781871409935307)
XLA Ops:
  0.0 1.3 slice.190
  1.6 1.3 slice.191
  3.5 2.4 collective-permute-start
  6.1 0.8 collective-permute-done
  7.5 1.3 maximum_convert_fusion.1
  8.8 11.8 %fusion.204 = bf16[2048,256]{1,0:T(8,128)(2,1)} fusion(f32[2048,262]{1,0:T(8,128)S(1)} %get-tuple-element.288, f32[2048,262]{1,0:T(8,128)S(1)} %get-tuple-element.287, f32[2048]{0:T(1024)S(1)} %bitcast.245, f32[2048]{0:T(1024)S(1)} %bitcast.244, f32[2048]{0:T(1024)S(1)} %bitcast.233, f32[2048]{0:T(1024)S(1)} %bitcast.234, f32[2048]{0:T(1024)S(1)} %bitcast.235, ...), kind=kLoop, calls=%fused_computation.203 | loop fusion | flops 14680064 | bytes 30523392 | tf_op jit(solution)/shard_map/convert_element_type | solution.py:125
  20.6 7.9 %all-to-all-start = ((bf16[8,256,256]{2,1,0:T(8,128)(2,1)}), bf16[8,256,256]{2,1,0:T(8,128)(2,1)S(1)}, u32[]{:S(2)}, u32[]{:S(2)}) async-start(bf16[8,256,256]{2,1,0:T(8,128)(2,1)} %bitcast.27), calls=%async_computation | async-start | bytes 2097152 | tf_op jit(solution)/shard_map/all_to_all | solution.py:126
  29.9 14.0 %all-to-all-done = bf16[8,256,256]{2,1,0:T(8,128)(2,1)S(1)} async-done(((bf16[8,256,256]{2,1,0:T(8,128)(2,1)}), bf16[8,256,256]{2,1,0:T(8,128)(2,1)S(1)}, u32[]{:S(2)}, u32[]{:S(2)}) %all-to-all-start) | async-done | bytes 1048608 | tf_op jit(solution)/shard_map/all_to_all | solution.py:126
  45.0 195.2 %while.12 = (s32[]{:T(128)}, bf16[16,16,2048]{2,1,0:T(8,128)(2,1)}, bf16[16,16,2048]{2,1,0:T(8,128)(2,1)S(1)}, bf16[16,16,2048]{2,1,0:T(8,128)(2,1)}, f32[16,16]{1,0:T(8,128)S(1)}, /*index=5*/s32[]{:T(128)}) while((s32[]{:T(128)}, bf16[16,16,2048]{2,1,0:T(8,128)(2,1)}, bf16[16,16,2048]{2,1,0:T(8,128)(2,1)S(1)}, ...), condition=%wide.region_1.2_spmd.clone.clone, body=%wide.region_0.1_spmd.clone.clone.sunk | while | flops 1256058880 | bytes 17597196 | solution.py:95
  45.1 0.9 dynamic-slice_bitcast_fusion.3
  57.2 0.8 dynamic-slice_bitcast_fusion.3
  69.5 0.8 dynamic-slice_bitcast_fusion.3
  81.6 0.8 dynamic-slice_bitcast_fusion.3
  93.8 0.8 dynamic-slice_bitcast_fusion.3
  106.0 0.8 dynamic-slice_bitcast_fusion.3
  118.2 0.8 dynamic-slice_bitcast_fusion.3
  130.4 0.8 dynamic-slice_bitcast_fusion.3
  142.6 0.8 dynamic-slice_bitcast_fusion.3
  154.8 0.8 dynamic-slice_bitcast_fusion.3
  167.0 0.8 dynamic-slice_bitcast_fusion.3
  179.2 0.8 dynamic-slice_bitcast_fusion.3
  191.4 0.8 dynamic-slice_bitcast_fusion.3
  203.6 0.8 dynamic-slice_bitcast_fusion.3
  215.8 0.8 dynamic-slice_bitcast_fusion.3
  228.0 0.8 dynamic-slice_bitcast_fusion.3
  240.2 1.5 copy.29
  241.8 1.2 copy.23
  242.9 4.2 %all-to-all-start.1 = ((bf16[256,8,256]{2,0,1:T(8,128)(2,1)}), bf16[256,8,256]{2,0,1:T(8,128)(2,1)}, u32[]{:S(2)}, u32[]{:S(2)}) async-start(bf16[256,8,256]{2,0,1:T(8,128)(2,1)} %copy.23), calls=%async_computation.1 | async-start | bytes 2097152 | tf_op jit(solution)/shard_map/all_to_all | solution.py:128
  247.2 1.1 copy.19
  248.3 2.0 maximum_convert_fusion
  250.3 12.3 %all-to-all-done.1 = bf16[256,8,256]{2,0,1:T(8,128)(2,1)} async-done(((bf16[256,8,256]{2,0,1:T(8,128)(2,1)}), bf16[256,8,256]{2,0,1:T(8,128)(2,1)}, u32[]{:S(2)}, u32[]{:S(2)}) %all-to-all-start.1) | async-done | bytes 1048608 | tf_op jit(solution)/shard_map/all_to_all | solution.py:128
  262.6 7.2 %fusion.223 = bf16[2048,256]{1,0:T(8,128)(2,1)} fusion(f32[2048,262]{1,0:T(8,128)S(1)} %maximum_convert_fusion, f32[2048]{0:T(1024)S(1)} %bitcast.225, f32[2048]{0:T(1024)S(1)} %bitcast.226, f32[2048]{0:T(1024)S(1)} %bitcast.227, f32[2048]{0:T(1024)S(1)} %bitcast.228, f32[2048]{0:T(1024)S(1)} %bitcast.229, f32[2048]{0:T(1024)S(1)} %bitcast.230, ...), kind=kLoop, calls=%fused_computation.243 | loop fusion | flops 9437184 | bytes 16834560 | tf_op jit(solution)/shard_map/convert_element_type | solution.py:107
  (472 shorter events, 182.4 us)
Async XLA Ops:
  0.0 3.1 %copy-start = (bf16[2048,256]{1,0:T(8,128)(2,1)S(1)}, bf16[2048,256]{1,0:T(8,128)(2,1)}, u32[]{:S(2)}) copy-start(bf16[2048,256]{1,0:T(8,128)(2,1)} %param.10) | copy-start | bytes 3145732
  1.3 4.6 %copy-start.2 = (f32[3,7,2048]{2,1,0:T(8,128)S(1)}, f32[3,7,2048]{2,1,0:T(8,128)}, u32[]{:S(2)}) copy-start(f32[3,7,2048]{2,1,0:T(8,128)} %param.11) | copy-start | bytes 516100
  2.8 4.7 %copy-start.1 = (bf16[2048,256]{1,0:T(8,128)(2,1)S(1)}, bf16[2048,256]{1,0:T(8,128)(2,1)}, u32[]{:S(2)}) copy-start(bf16[2048,256]{1,0:T(8,128)(2,1)} %param.9) | copy-start | bytes 3145732
  3.5 3.3 %collective-permute-start = (bf16[3,2048,6]{1,2,0:T(8,128)(2,1)S(1)}, bf16[3,2048,6]{1,2,0:T(8,128)(2,1)S(1)}, u32[]{:S(2)}, u32[]{:S(2)}) collective-permute-start(bf16[3,2048,6]{1,2,0:T(8,128)(2,1)S(1)} %pad_maximum_fusion), channel_id=1, source_target_pairs={{0,4},{4,8},{8,12},{12,16},{16,20},{20,24},{24,28},{1,5},{5,9},{9,... | collective-permute-start | bytes 221192 | tf_op jit(solution)/shard_map/ppermute | solution.py:13
  20.6 8.5 %copy-start.3 = (f32[1,256]{1,0:T(1,128)S(1)}, f32[1,256]{1,0:T(1,128)}, u32[]{:S(2)}) copy-start(f32[1,256]{1,0:T(1,128)} %param.13) | copy-start | bytes 3076
  20.6 23.3 %all-to-all-start = ((bf16[8,256,256]{2,1,0:T(8,128)(2,1)}), bf16[8,256,256]{2,1,0:T(8,128)(2,1)S(1)}, u32[]{:S(2)}, u32[]{:S(2)}) async-start(bf16[8,256,256]{2,1,0:T(8,128)(2,1)} %bitcast.27), calls=%async_computation | async-start | bytes 2097152 | tf_op jit(solution)/shard_map/all_to_all | solution.py:126
  242.9 19.6 %all-to-all-start.1 = ((bf16[256,8,256]{2,0,1:T(8,128)(2,1)}), bf16[256,8,256]{2,0,1:T(8,128)(2,1)}, u32[]{:S(2)}, u32[]{:S(2)}) async-start(bf16[256,8,256]{2,0,1:T(8,128)(2,1)} %copy.23), calls=%async_computation.1 | async-start | bytes 2097152 | tf_op jit(solution)/shard_map/all_to_all | solution.py:128
where the time goes:
time: 271 us; the launch traced here: 270 us
  matrix products  164 us (61%)
  other arithmetic  35.8 us (13%)
  waiting for transfers between devices  27 us (10%)
  local copies, waits for them, and re-layouts  24.4 us (9%)
  starting transfers between devices  14.6 us (5%)
  loops' own time  3.38 us (1%)
    dot_general x32, matrix products, forward(): jnp.einsum('ckb,bm->ckm', twist_re, sin_cols, precision=HIGH)  20.2 us
    dot_general x32, matrix products, forward(): jnp.einsum('ckb,bm->ckm', twist_im, sin_cols, precision=HIGH)  19.7 us
    dot_general x32, matrix products, forward(): jnp.einsum('ckb,bm->ckm', twist_im, cos_cols, precision=HIGH)  19.5 us
    dot_general x32, matrix products, forward(): jnp.einsum('ckb,bm->ckm', twist_re, cos_cols, precision=HIGH)  19.5 us
    dot_general x64, matrix products, first_section(): jnp.einsum('ka,cab->ckb', table_rest, shaped, preferred_element_type=jnp....  17.9 us
    dot_general x64, matrix products, first_section(): jnp.einsum('ka,cab->ckb', table_head, shaped, preferred_element_type=jnp....  17.5 us
    all_to_all x1, waiting for transfers between devices, local(): lax.all_to_all(gated, 'ctx', split_axis=0, concat_axis=1, tiled=True)  14 us
    while x48, local copies, waits for them, and re-layouts  14 us
  transfers between devices with their start and end apart: 3, of which 3 were waited for; matrix products, arithmetic and copies ran while one was open for 2% of the time, Pallas kernels for 0%

commit v1 on v0

--- a/solution.py
+++ b/solution.py
@@ -5,6 +5,18 @@
 from jax.sharding import PartitionSpec as P
 
 HIGH = lax.Precision.HIGHEST
+
+
+def split_up(shard, dim, devices):
+    shape = shard.shape
+    blocks = shard.reshape(*shape[:dim], devices, shape[dim] // devices, *shape[dim + 1 :])
+    return jnp.moveaxis(blocks, dim, 0)
+
+
+def joined_along(blocks, dim):
+    blocks = jnp.moveaxis(blocks, 0, dim)
+    lengths = blocks.shape
+    return blocks.reshape(*lengths[:dim], lengths[dim] * lengths[dim + 1], *lengths[dim + 2 :])
 
 
 def passed_along(value, axis, by):
@@ -123,7 +135,16 @@
         short_conv(extend_home(keys, 1), short_taps[1], tok_local)
         * short_conv(extend_home(values, 2), short_taps[2], tok_local)
     ).astype(jnp.bfloat16)
-    g_owned = lax.all_to_all(gated, "ctx", split_axis=0, concat_axis=1, tiled=True)
+    peers_2, mine = (lax.axis_size("ctx"), lax.axis_index("ctx"))
+    blocks_2 = split_up(gated, 0, peers_2)
+    outs = [blocks_2[mine]]
+    for step in range(1, peers_2):
+        sent = blocks_2[(mine + step) % peers_2]
+        outs.append(
+            lax.ppermute(sent, "ctx", [(i_2, (i_2 + step) % peers_2) for i_2 in range(peers_2)])
+        )
+    blocks_2 = jnp.stack(outs)[(mine - jnp.arange(peers_2)) % peers_2]
+    g_owned = joined_along(blocks_2, 1)
     outgoing = long_conv(g_owned, long_filter[0], skip_gain[0])
     returned = lax.all_to_all(outgoing, "ctx", split_axis=1, concat_axis=0, tiled=True)
     return gate_product(q_short, returned)

time: 271 us -> 257 us (0.948)
  other arithmetic: 35.8 us -> 24.8 us
  waiting for transfers between devices: 27 us -> 17.8 us
  starting transfers between devices: 14.6 us -> 21 us
    all_to_all x1 -> x0, waiting for transfers between devices: 14 us -> none  [local(): lax.all_to_all(gated, 'ctx', split_axis=0, concat_axis=1, tiled=True)]
    ppermute x0 -> x7, starting transfers between devices: none -> 13.6 us  [local(): lax.ppermute(sent, 'ctx', [(i_2, (i_2 + step) % peers_2) for i_2 in range...]
    dynamic_update_slice x16, other arithmetic: 11.5 us -> 1.36 us  [long_conv(): lax.map(one_block, (gated.reshape(count, block, length), filters.reshape(...]
    all_to_all x1 -> x0, starting transfers between devices: 7.94 us -> none  [local(): lax.all_to_all(gated, 'ctx', split_axis=0, concat_axis=1, tiled=True)]
    ppermute x0 -> x7, waiting for transfers between devices: none -> 4.48 us  [local(): lax.ppermute(sent, 'ctx', [(i_2, (i_2 + step) % peers_2) for i_2 in range...]
  transfers between devices with their start and end apart: 3 -> 9, of which waited for: 3 -> 5; matrix products, arithmetic and copies ran while one was open for 2% -> 2% of each run, Pallas kernels for 0% -> 0%
where the time goes in v1:
time: 257 us; the launch traced here: 256 us
  matrix products  165 us (64%)
  other arithmetic  24.8 us (10%)
  local copies, waits for them, and re-layouts  24 us (9%)
  starting transfers between devices  21 us (8%)
  waiting for transfers between devices  17.8 us (7%)
  loops' own time  3.65 us (1%)
    dot_general x32, matrix products, forward(): jnp.einsum('ckb,bm->ckm', twist_re, sin_cols, precision=HIGH)  20.2 us
    dot_general x32, matrix products, forward(): jnp.einsum('ckb,bm->ckm', twist_im, sin_cols, precision=HIGH)  19.8 us
    dot_general x32, matrix products, forward(): jnp.einsum('ckb,bm->ckm', twist_im, cos_cols, precision=HIGH)  19.5 us
    dot_general x32, matrix products, forward(): jnp.einsum('ckb,bm->ckm', twist_re, cos_cols, precision=HIGH)  19.5 us
    dot_general x64, matrix products, first_section(): jnp.einsum('ka,cab->ckb', table_rest, shaped, preferred_element_type=jnp....  17.9 us
    dot_general x64, matrix products, first_section(): jnp.einsum('ka,cab->ckb', table_head, shaped, preferred_element_type=jnp....  17.5 us
    while x48, local copies, waits for them, and re-layouts  14 us
    ppermute x7, starting transfers between devices, local(): lax.ppermute(sent, 'ctx', [(i_2, (i_2 + step) % peers_2) for i_2 in range...  13.6 us
  transfers between devices with their start and end apart: 9, of which 5 were waited for; matrix products, arithmetic and copies ran while one was open for 2% of the time, Pallas kernels for 0%

profile of v1, /device:TPU:0, one launch (start us, length us, event | category | flops | bytes accessed | tf_op | source)
XLA Modules:
  0.0 256.1 jit_solution(846500179866727178)
XLA Ops:
  0.0 1.3 slice.190
  1.6 1.3 slice.191
  3.5 2.4 collective-permute-start
  7.5 1.3 maximum_convert_fusion.1
  8.8 11.1 %fusion.204 = bf16[2048,256]{1,0:T(8,128)(2,1)S(1)} fusion(f32[2048,262]{1,0:T(8,128)S(1)} %get-tuple-element.296, f32[2048,262]{1,0:T(8,128)S(1)} %get-tuple-element.295, f32[2048]{0:T(1024)S(1)} %bitcast.278, f32[2048]{0:T(1024)S(1)} %bitcast.277, f32[2048]{0:T(1024)S(1)} %bitcast.266, f32[2048]{0:T(1024)S(1)} %bitcast.267, f32[2048]{0:T(1024)S(1)} %bitcast.268, ...), kind=kLoop, calls=%fused_computation.204 | loop fusion | flops 14680064 | bytes 30523392 | tf_op jit(solution)/shard_map/convert_element_type | solution.py:137
  20.0 3.3 %collective-permute-start.1 = (bf16[256,256]{1,0:T(8,128)(2,1)S(1)}, bf16[256,256]{1,0:T(8,128)(2,1)S(1)}, u32[]{:S(2)}, u32[]{:S(2)}) collective-permute-start(bf16[256,256]{1,0:T(8,128)(2,1)S(1)} %get-tuple-element.269), channel_id=1, source_target_pairs={{0,4},{4,8},{8,12},{12,16},{16,20},{20,24},{24,28},{28,0},{1,5},{5... | collective-permute-start | bytes 393224 | tf_op jit(solution)/shard_map/ppermute | solution.py:144
  24.6 2.4 collective-permute-start.2
  26.9 2.4 collective-permute-start.3
  30.5 1.8 collective-permute-start.6
  32.3 2.6 %collective-permute-start.7 = (bf16[256,256]{1,0:T(8,128)(2,1)S(1)}, bf16[256,256]{1,0:T(8,128)(2,1)S(1)}, u32[]{:S(2)}, u32[]{:S(2)}) collective-permute-start(bf16[256,256]{1,0:T(8,128)(2,1)S(1)} %get-tuple-element.263), channel_id=1, source_target_pairs={{0,28},{4,0},{8,4},{12,8},{16,12},{20,16},{24,20},{28,24},{1,29},{... | collective-permute-start | bytes 393224 | tf_op jit(solution)/shard_map/ppermute | solution.py:144
  34.9 0.9 collective-permute-done.3
  35.8 1.3 collective-permute-done.4
  37.1 2.2 collective-permute-done.5
  41.2 185.5 %while.12 = (s32[]{:T(128)}, bf16[16,16,2048]{2,1,0:T(8,128)(2,1)S(1)}, bf16[16,16,2048]{2,1,0:T(8,128)(2,1)S(1)}, bf16[16,16,2048]{2,1,0:T(8,128)(2,1)}, f32[16,16]{1,0:T(8,128)S(1)}, /*index=5*/s32[]{:T(128)}) while((s32[]{:T(128)}, bf16[16,16,2048]{2,1,0:T(8,128)(2,1)S(1)}, bf16[16,16,2048]{2,1,0:T(8,128)(2,1)S(1)}, ...), condition=%wide.region_1.2_spmd.clone.clone, body=%wide.region_0.1_spmd.clone.clone.sunk | while | flops 1256058880 | bytes 17597136 | solution.py:107
  41.2 0.9 dynamic-slice_bitcast_fusion.10
  52.8 0.9 dynamic-slice_bitcast_fusion.10
  64.4 0.9 dynamic-slice_bitcast_fusion.10
  76.0 0.9 dynamic-slice_bitcast_fusion.10
  87.6 0.9 dynamic-slice_bitcast_fusion.10
  99.2 0.9 dynamic-slice_bitcast_fusion.10
  110.8 0.9 dynamic-slice_bitcast_fusion.10
  122.4 0.9 dynamic-slice_bitcast_fusion.10
  134.0 0.9 dynamic-slice_bitcast_fusion.10
  145.6 0.9 dynamic-slice_bitcast_fusion.10
  157.2 0.9 dynamic-slice_bitcast_fusion.10
  168.7 0.9 dynamic-slice_bitcast_fusion.10
  227.0 1.2 copy.18
  228.2 5.0 %all-to-all-start = ((bf16[256,8,256]{2,0,1:T(8,128)(2,1)}), bf16[256,8,256]{2,0,1:T(8,128)(2,1)}, u32[]{:S(2)}, u32[]{:S(2)}) async-start(bf16[256,8,256]{2,0,1:T(8,128)(2,1)} %copy.18), calls=%async_computation | async-start | bytes 2097152 | tf_op jit(solution)/shard_map/all_to_all | solution.py:149
  233.2 1.1 copy.14
  234.3 2.0 maximum_convert_fusion
  236.3 12.6 %all-to-all-done = bf16[256,8,256]{2,0,1:T(8,128)(2,1)} async-done(((bf16[256,8,256]{2,0,1:T(8,128)(2,1)}), bf16[256,8,256]{2,0,1:T(8,128)(2,1)}, u32[]{:S(2)}, u32[]{:S(2)}) %all-to-all-start) | async-done | bytes 1048608 | tf_op jit(solution)/shard_map/all_to_all | solution.py:149
  248.9 7.2 %fusion.223 = bf16[2048,256]{1,0:T(8,128)(2,1)} fusion(f32[2048,262]{1,0:T(8,128)S(1)} %maximum_convert_fusion, f32[2048]{0:T(1024)S(1)} %bitcast.258, f32[2048]{0:T(1024)S(1)} %bitcast.259, f32[2048]{0:T(1024)S(1)} %bitcast.260, f32[2048]{0:T(1024)S(1)} %bitcast.261, f32[2048]{0:T(1024)S(1)} %bitcast.262, f32[2048]{0:T(1024)S(1)} %bitcast.263, ...), kind=kLoop, calls=%fused_computation.244 | loop fusion | flops 9437184 | bytes 16834560 | tf_op jit(solution)/shard_map/convert_element_type | solution.py:119
  (495 shorter events, 178.5 us)
Async XLA Ops:
  0.0 3.1 %copy-start = (bf16[2048,256]{1,0:T(8,128)(2,1)S(1)}, bf16[2048,256]{1,0:T(8,128)(2,1)}, u32[]{:S(2)}) copy-start(bf16[2048,256]{1,0:T(8,128)(2,1)} %param.10) | copy-start | bytes 3145732
  1.3 4.6 %copy-start.2 = (f32[3,7,2048]{2,1,0:T(8,128)S(1)}, f32[3,7,2048]{2,1,0:T(8,128)}, u32[]{:S(2)}) copy-start(f32[3,7,2048]{2,1,0:T(8,128)} %param.11) | copy-start | bytes 516100
  2.8 4.7 %copy-start.1 = (bf16[2048,256]{1,0:T(8,128)(2,1)S(1)}, bf16[2048,256]{1,0:T(8,128)(2,1)}, u32[]{:S(2)}) copy-start(bf16[2048,256]{1,0:T(8,128)(2,1)} %param.9) | copy-start | bytes 3145732
  3.5 3.3 %collective-permute-start = (bf16[3,2048,6]{1,2,0:T(8,128)(2,1)S(1)}, bf16[3,2048,6]{1,2,0:T(8,128)(2,1)S(1)}, u32[]{:S(2)}, u32[]{:S(2)}) collective-permute-start(bf16[3,2048,6]{1,2,0:T(8,128)(2,1)S(1)} %pad_maximum_fusion), channel_id=1, source_target_pairs={{0,4},{4,8},{8,12},{12,16},{16,20},{20,24},{24,28},{1,5},{5,9},{9,... | collective-permute-start | bytes 221192 | tf_op jit(solution)/shard_map/ppermute | solution.py:25
  19.9 4.0 %copy-start.3 = (f32[1,256]{1,0:T(1,128)S(1)}, f32[1,256]{1,0:T(1,128)}, u32[]{:S(2)}) copy-start(f32[1,256]{1,0:T(1,128)} %param.13) | copy-start | bytes 3076
  20.0 10.5 %collective-permute-start.1 = (bf16[256,256]{1,0:T(8,128)(2,1)S(1)}, bf16[256,256]{1,0:T(8,128)(2,1)S(1)}, u32[]{:S(2)}, u32[]{:S(2)}) collective-permute-start(bf16[256,256]{1,0:T(8,128)(2,1)S(1)} %get-tuple-element.269), channel_id=1, source_target_pairs={{0,4},{4,8},{8,12},{12,16},{16,20},{20,24},{24,28},{28,0},{1,5},{5... | collective-permute-start | bytes 393224 | tf_op jit(solution)/shard_map/ppermute | solution.py:144
  24.6 7.7 %collective-permute-start.2 = (bf16[256,256]{1,0:T(8,128)(2,1)S(1)}, bf16[256,256]{1,0:T(8,128)(2,1)S(1)}, u32[]{:S(2)}, u32[]{:S(2)}) collective-permute-start(bf16[256,256]{1,0:T(8,128)(2,1)S(1)} %get-tuple-element.268), channel_id=1, source_target_pairs={{0,8},{4,12},{8,16},{12,20},{16,24},{20,28},{24,0},{28,4},{1,9},{5... | collective-permute-start | bytes 393224 | tf_op jit(solution)/shard_map/ppermute | solution.py:144
  26.9 8.9 %collective-permute-start.3 = (bf16[256,256]{1,0:T(8,128)(2,1)S(1)}, bf16[256,256]{1,0:T(8,128)(2,1)S(1)}, u32[]{:S(2)}, u32[]{:S(2)}) collective-permute-start(bf16[256,256]{1,0:T(8,128)(2,1)S(1)} %get-tuple-element.267), channel_id=1, source_target_pairs={{0,12},{4,16},{8,20},{12,24},{16,28},{20,0},{24,4},{28,8},{1,13},{... | collective-permute-start | bytes 393224 | tf_op jit(solution)/shard_map/ppermute | solution.py:144
  29.3 7.8 %collective-permute-start.4 = (bf16[256,256]{1,0:T(8,128)(2,1)S(1)}, bf16[256,256]{1,0:T(8,128)(2,1)S(1)}, u32[]{:S(2)}, u32[]{:S(2)}) collective-permute-start(bf16[256,256]{1,0:T(8,128)(2,1)S(1)} %get-tuple-element.266), channel_id=1, source_target_pairs={{0,16},{4,20},{8,24},{12,28},{16,0},{20,4},{24,8},{28,12},{1,17},{... | collective-permute-start | bytes 393224 | tf_op jit(solution)/shard_map/ppermute | solution.py:144
  29.8 9.5 %collective-permute-start.5 = (bf16[256,256]{1,0:T(8,128)(2,1)S(1)}, bf16[256,256]{1,0:T(8,128)(2,1)S(1)}, u32[]{:S(2)}, u32[]{:S(2)}) collective-permute-start(bf16[256,256]{1,0:T(8,128)(2,1)S(1)} %get-tuple-element.265), channel_id=1, source_target_pairs={{0,20},{4,24},{8,28},{12,0},{16,4},{20,8},{24,12},{28,16},{1,21},{... | collective-permute-start | bytes 393224 | tf_op jit(solution)/shard_map/ppermute | solution.py:144
  30.5 8.9 %collective-permute-start.6 = (bf16[256,256]{1,0:T(8,128)(2,1)S(1)}, bf16[256,256]{1,0:T(8,128)(2,1)S(1)}, u32[]{:S(2)}, u32[]{:S(2)}) collective-permute-start(bf16[256,256]{1,0:T(8,128)(2,1)S(1)} %get-tuple-element.264), channel_id=1, source_target_pairs={{0,24},{4,28},{8,0},{12,4},{16,8},{20,12},{24,16},{28,20},{1,25},{... | collective-permute-start | bytes 393224 | tf_op jit(solution)/shard_map/ppermute | solution.py:144
  32.3 7.1 %collective-permute-start.7 = (bf16[256,256]{1,0:T(8,128)(2,1)S(1)}, bf16[256,256]{1,0:T(8,128)(2,1)S(1)}, u32[]{:S(2)}, u32[]{:S(2)}) collective-permute-start(bf16[256,256]{1,0:T(8,128)(2,1)S(1)} %get-tuple-element.263), channel_id=1, source_target_pairs={{0,28},{4,0},{8,4},{12,8},{16,12},{20,16},{24,20},{28,24},{1,29},{... | collective-permute-start | bytes 393224 | tf_op jit(solution)/shard_map/ppermute | solution.py:144
  228.2 20.7 %all-to-all-start = ((bf16[256,8,256]{2,0,1:T(8,128)(2,1)}), bf16[256,8,256]{2,0,1:T(8,128)(2,1)}, u32[]{:S(2)}, u32[]{:S(2)}) async-start(bf16[256,8,256]{2,0,1:T(8,128)(2,1)} %copy.18), calls=%async_computation | async-start | bytes 2097152 | tf_op jit(solution)/shard_map/all_to_all | solution.py:149
